TPU v7x, 32 devices: a whole 2x2x4 slice. The times are simulated.
32 devices in a mesh: seq: 8 (over z, x), head: 4 (over y, core).
Axes of the slice: x: 2, y: 2, z: 4, core: 2. Of those that a mesh axis runs over, the one named last changes fastest.
Arguments:
- lin_query: bfloat16 [2048, 4096], P('seq', 'head'), may hold values from -2 to 2
- lin_key: bfloat16 [2048, 4096], P('seq', 'head'), may hold values from -2 to 2
- lin_value: bfloat16 [2048, 4096], P('seq', 'head'), may hold values from -130 to 130
- log_decay: float32 [2048, 32], P('seq', 'head'), may hold values from -2 to 0
- gate_logits: bfloat16 [2048, 4096], P('seq', 'head'), may hold values from -6 to 6
- norm_gain: float32 [4096], P('head'), may hold values from 0.25 to 1.75
- soft_query: bfloat16 [2048, 4096], P('seq', 'head'), may hold values from -4 to 4
- soft_key: bfloat16 [2048, 4096], P('seq', 'head'), may hold values from -4 to 4
- soft_value: bfloat16 [2048, 4096], P('seq', 'head'), may hold values from -6 to 6
- doc_ids: int32 [2048], P('seq'), may hold values from 0 to 8, as said below
- doc_spans: int32 [9, 2], replicated, may hold values from 0 to 2048, as said below
Outputs:
- lin_out: bfloat16 [2048, 4096], P('seq', 'head')
- soft_out: bfloat16 [2048, 4096], P('seq', 'head')
Inputs may be any that keep to these rules, and one draw needn't show every extreme that they name: `doc_ids`: never falls; document d covers exactly the positions doc_spans[d, 0] to doc_spans[d, 1] - 1. `doc_spans`: row 0 starts at 0, each row ends where the next starts, the last ends at 2048; every document holds 1 to 768 positions, and one holds exactly that many.
All inputs are finite; a program needn't handle non-finite values.
Results may differ from a plain program's by a relative error of at most 0.0053.
Values may be sent and summed in bfloat16 or wider, within the bound.
No kernel may reach another device: no remote copies, remote signals or barrier semaphores. Data moves between devices by JAX's collectives and lax.ppermute only.
A program may use at most 128 MiB of HBM per device.

v0:
```python
import jax
import jax.numpy as jnp
from jax import lax
from jax.sharding import PartitionSpec as P

HALF_MODEL_HEADS = 32
HD = 128
SPAN = 3


def entering(part, axis, combine, identity):
    place = lax.axis_index(axis)
    gathered = jax.tree.map(lambda a: lax.all_gather(a, axis), part)
    state = jax.tree.map(lambda a, e: jnp.zeros_like(a) + jnp.asarray(e, a.dtype), part, identity)

    def one(step, state):
        return combine(
            state, jax.tree.map(lambda a: lax.dynamic_index_in_dim(a, step, 0, False), gathered)
        )

    return lax.fori_loop(0, place, one, state)


def from_behind(array, axis, by):
    devices = lax.axis_size(axis)
    pairs = [(i, i + by) for i in range(devices) if 0 <= i + by < devices]
    return lax.ppermute(array, axis, pairs)


def combine(former, latter):
    return (former[0] * latter[0], latter[0][:, None, None] * former[1] + latter[1])


def shards(
    lin_query,
    lin_key,
    lin_value,
    log_decay,
    gate_logits,
    norm_gain,
    soft_query,
    soft_key,
    soft_value,
    doc_ids,
    doc_spans,
):
    token_rows = lin_query.shape[0]
    feature_width = lin_query.shape[1]
    head_count = feature_width // HD
    block_base = lax.axis_index("seq") * token_rows
    positions = block_base + jnp.arange(token_rows, dtype=jnp.int32)
    numbers = jnp.arange(doc_spans.shape[0], dtype=jnp.int32)
    starts = jnp.sum(
        jnp.where(doc_ids[:, None] == numbers[None, :], doc_spans[None, :, 0], 0), axis=1
    )
    queries = lin_query.reshape(token_rows, head_count, HD)
    key_rows = lin_key.reshape(token_rows, head_count, HD)
    value_rows = lin_value.reshape(token_rows, head_count, HD)
    cumulative = jnp.cumsum(log_decay, axis=0)
    scores = jnp.einsum("thd,shd->hts", queries, key_rows, preferred_element_type=jnp.float32)
    spread = cumulative.T[:, :, None] - cumulative.T[:, None, :]
    allowed = (positions[None, :] <= positions[:, None]) & (positions[None, :] >= starts[:, None])
    weights = jnp.where(allowed[None], scores * jnp.exp(jnp.minimum(spread, 0.0)), 0.0).astype(
        jnp.bfloat16
    )
    inner_part = jnp.einsum("hts,shd->thd", weights, value_rows, preferred_element_type=jnp.float32)
    last_cumul = cumulative[-1]
    tail_weight = jnp.where(
        (positions >= starts[-1])[:, None],
        jnp.exp(jnp.minimum(last_cumul[None, :] - cumulative, 0.0)),
        0.0,
    )
    tail_key = (key_rows.astype(jnp.float32) * tail_weight[:, :, None]).astype(jnp.bfloat16)
    local_state = jnp.einsum(
        "shd,she->hde", tail_key, value_rows, preferred_element_type=jnp.float32
    )
    local_decay = jnp.where(starts[-1] < block_base, jnp.exp(last_cumul), 0.0)
    entry_scale = jnp.where((starts < block_base)[:, None], jnp.exp(cumulative), 0.0)
    identity = (jnp.ones_like(local_decay), jnp.zeros_like(local_state))
    carried = entering((local_decay, local_state), "seq", combine, identity)[1]
    cross_part = (
        jnp.einsum(
            "thd,hde->the",
            queries,
            carried.astype(jnp.bfloat16),
            preferred_element_type=jnp.float32,
        )
        * entry_scale[:, :, None]
    )
    mixture = inner_part + cross_part
    squares = jnp.sum(mixture * mixture, axis=(1, 2))
    norm_total = lax.psum(squares, "head")
    norm_scale = lax.rsqrt(norm_total / (HALF_MODEL_HEADS * HD) + 1e-06)
    lin_out = (
        mixture.reshape(token_rows, feature_width)
        * norm_scale[:, None]
        * norm_gain[None, :]
        * jax.nn.sigmoid(gate_logits.astype(jnp.float32))
    ).astype(jnp.bfloat16)
    key_parts = [soft_key]
    value_parts = [soft_value]
    for distance in range(1, SPAN + 1):
        earlier = from_behind((soft_key, soft_value), "seq", distance)
        key_parts.insert(0, earlier[0])
        value_parts.insert(0, earlier[1])
    all_keys = jnp.concatenate(key_parts, axis=0)
    all_values = jnp.concatenate(value_parts, axis=0)
    span_rows = all_keys.shape[0]
    key_pos = block_base + token_rows - span_rows + jnp.arange(span_rows, dtype=jnp.int32)
    soft_queries = soft_query.reshape(token_rows, head_count, HD)
    logits = jnp.einsum(
        "thd,shd->hts",
        soft_queries,
        all_keys.reshape(span_rows, head_count, HD),
        preferred_element_type=jnp.float32,
    ) * HD ** (-0.5)
    visible = (key_pos[None, :] >= starts[:, None]) & (key_pos[None, :] <= positions[:, None])
    logits = jnp.where(visible[None], logits, -jnp.inf)
    row_max = jnp.max(logits, axis=2, keepdims=True)
    soft_weights = jnp.exp(logits - row_max)
    soft_total = jnp.sum(soft_weights, axis=2)
    attended = jnp.einsum(
        "hts,shd->thd",
        soft_weights.astype(jnp.bfloat16),
        all_values.reshape(span_rows, head_count, HD),
        preferred_element_type=jnp.float32,
    )
    soft_out = (
        (attended / soft_total.T[:, :, None])
        .reshape(token_rows, feature_width)
        .astype(jnp.bfloat16)
    )
    return (lin_out, soft_out)


def solution(mesh):
    in_specs = (
        P("seq", "head"),
        P("seq", "head"),
        P("seq", "head"),
        P("seq", "head"),
        P("seq", "head"),
        P("head"),
        P("seq", "head"),
        P("seq", "head"),
        P("seq", "head"),
        P("seq"),
        P(),
    )
    out_specs = (P("seq", "head"), P("seq", "head"))
    return jax.shard_map(shards, mesh=mesh, in_specs=in_specs, out_specs=out_specs, check_vma=False)
```

profile of v0, /device:TPU:30, one launch (start us, length us, event | category | flops | bytes accessed | tf_op | source)
XLA Modules:
  0.0 212.4 jit_solution(500775631223508674)
XLA Ops:
  10.7 1.3 reduce-window.6
  12.1 1.2 copy.96
  13.7 2.1 %fusion.22 = f32[8,128,128]{2,1,0:T(8,128)} fusion(bf16[256,8,128]{0,2,1:T(8,128)(2,1)S(1)} %bitcast.97, f32[256,8]{0,1:T(8,128)S(1)} %exponential_select_fusion.1, bf16[256,1024]{1,0:T(8,128)(2,1)} %param.15), kind=kOutput, calls=%fused_computation.30 | convolution fusion | flops 67895296 | bytes 1581056 | tf_op jit(solution)/shard_map/shd,she->hde/dot_general | solution.py:74
  15.9 2.1 copy.85
  17.9 1.3 collective-permute-start.3
  19.2 1.3 collective-permute-start.4
  20.5 1.3 collective-permute-start
  21.8 1.3 collective-permute-start.1
  23.1 1.3 collective-permute-start.2
  24.4 136.3 %all-gather.1 = f32[8,1,8]{2,1,0:T(1,128)S(1)} all-gather(f32[1,1,8]{2,1,0:T(1,128)S(1)} %bitcast.106), channel_id=1, replica_groups=mesh['seq'=8,'head'=4] {'seq'}, dimensions={0}, use_global_device_ids=true | all-gather | bytes 288 | tf_op jit(solution)/shard_map/all_gather | solution.py:13
  160.9 1.3 collective-permute-start.5
  163.3 1.7 pad_maximum_fusion
  165.0 2.6 %copy.84 = bf16[1024,1024]{0,1:T(8,128)(2,1)} copy(bf16[1024,1024]{1,0:T(8,128)(2,1)S(1)} %pad_maximum_fusion) | data formatting | bytes 4194304 | tf_op jit(solution)/shard_map/concatenate | solution.py:107
  167.6 6.7 %collective-permute-done.5 = bf16[256,1024]{0,1:T(8,128)(2,1)} collective-permute-done((bf16[256,1024]{0,1:T(8,128)(2,1)}, bf16[256,1024]{0,1:T(8,128)(2,1)}, u32[]{:S(2)}, u32[]{:S(2)}) %collective-permute-start.5) | collective-permute-done | bytes 524320 | tf_op jit(solution)/shard_map/ppermute | solution.py:27
  174.4 1.8 pad_maximum_fusion.1
  176.2 1.7 fusion.2
  177.9 1.7 fusion
  179.6 2.2 %divide_convert_fusion = bf16[256,8,128]{0,2,1:T(8,128)(2,1)S(1)} fusion(bf16[1024,8,128]{0,2,1:T(8,128)(2,1)S(1)} %bitcast.99, f32[8,1024,256]{2,1,0:T(8,128)S(1)} %get-tuple-element.74, f32[8,256]{1,0:T(8,128)S(1)} %get-tuple-element.73, pred[256,1024]{0,1:T(8,128)(4,1)S(1)} %compare_and_fusion, f32[256,8]{0,1:T(8,128)S(1)} %bitcast.104), kind=kOutput, calls=%fused_computation.21 | convolution fusion | flops 545783808 | bytes 11288576 | tf_op jit(solution)/shard_map/hts,shd->thd/dot_general | solution.py:122
  182.9 8.7 %while.12 = (s32[]{:T(128)}, f32[8,128,128]{2,1,0:T(8,128)S(1)}, s32[]{:T(128)}, f32[8,8]{1,0:T(8,128)S(1)}, f32[8,8,128,128]{3,2,1,0:T(8,128)}, /*index=5*/s32[]{:T(128)}, s32[]{:T(128)}, s32[]{:T(128)}) while((s32[]{:T(128)}, f32[8,128,128]{2,1,0:T(8,128)S(1)}, s32[]{:T(128)}, f32[8,8]{1,0:T(8,128)S(1)}, f32[8,8,128,128]{3,2,1,0:T(8,128)}, ...), condition=%wide.region_4.5_spmd, body=%wide.region_3.4_spmd.sunk | while | flops 262149 | bytes 1573087 | solution.py:21
  191.6 1.4 fusion.12
  193.0 2.9 %multiply_reduce_fusion = (f32[256]{0:T(256)S(1)}, f32[256,8,128]{0,2,1:T(8,128)}) fusion(f32[256,8,128]{0,2,1:T(8,128)S(1)} %fusion.12, bf16[256,8,128]{0,2,1:T(8,128)(2,1)S(1)} %bitcast.98, f32[8,256]{1,0:T(8,128)S(1)} %add_bitcast_fusion.1, pred[256,256]{1,0:T(8,128)(4,1)S(1)} %compare_and_fusion.1, bf16[256,1024]{1,0:T(8,128)(2,1)S(1)} %copy-done.2, ...), kind=kOutput, calls=%fused_computation.23 | convolution fusion | flops 271843072 | bytes 3744768 | tf_op jit(solution)/shard_map/hts,shd->thd/dot_general | solution.py:66
  195.9 1.6 copy.83
  197.5 5.9 %psum.7 = f32[256]{0:T(256)S(1)} all-reduce(f32[256]{0:T(256)S(1)} %get-tuple-element.71), channel_id=1, replica_groups=mesh['seq'=8,'head'=4] {'head'}, use_global_device_ids=true, to_apply=%region_6.7 | all-reduce | flops 256 | bytes 2048 | tf_op jit(solution)/shard_map/psum | solution.py:92
  203.4 2.2 %multiply_convert_fusion = bf16[256,1024]{1,0:T(8,128)(2,1)} fusion(bf16[256,1024]{1,0:T(8,128)(2,1)} %param.17, f32[256,1024]{1,0:T(8,128)S(1)} %copy.83, f32[1024]{0:T(1024)S(1)} %copy-done.6, f32[256]{0:T(256)S(1)} %add_rsqrt_fusion), kind=kLoop, calls=%fused_computation.22 | loop fusion | flops 2097152 | bytes 2102272 | tf_op jit(solution)/shard_map/convert_element_type | solution.py:99
  (54 shorter events, 14.2 us)
Async XLA Ops:
  7.2 169.0 %copy-start = (bf16[256,1024]{1,0:T(8,128)(2,1)S(1)}, bf16[256,1024]{1,0:T(8,128)(2,1)}, u32[]{:S(2)}) copy-start(bf16[256,1024]{1,0:T(8,128)(2,1)} %param.19) | copy-start | bytes 1572868
  7.2 13.3 %copy-start.3 = (bf16[256,1024]{1,0:T(8,128)(2,1)S(1)}, bf16[256,1024]{1,0:T(8,128)(2,1)}, u32[]{:S(2)}) copy-start(bf16[256,1024]{1,0:T(8,128)(2,1)} %param.21) | copy-start | bytes 1572868
  7.2 175.6 %all-gather.4.cloned.1.call-start = ((), (), s32[]{:S(2)}) async-start(), calls=%async_computation | async-start | bytes 4718592 | tf_op jit(solution)/shard_map/all_gather | solution.py:13
  17.9 149.7 %collective-permute-start.3 = (bf16[256,1024]{0,1:T(8,128)(2,1)}, bf16[256,1024]{0,1:T(8,128)(2,1)}, u32[]{:S(2)}, u32[]{:S(2)}) collective-permute-start(bf16[256,1024]{0,1:T(8,128)(2,1)} %copy.85), channel_id=1, source_target_pairs={{0,12},{4,16},{8,20},{12,24},{16,28},{1,13},{5,17},{9,21},{13,25},... | collective-permute-start | bytes 1572872 | tf_op jit(solution)/shard_map/ppermute | solution.py:27
  19.2 148.4 %collective-permute-start.4 = (bf16[256,1024]{0,1:T(8,128)(2,1)}, bf16[256,1024]{0,1:T(8,128)(2,1)}, u32[]{:S(2)}, u32[]{:S(2)}) collective-permute-start(bf16[256,1024]{0,1:T(8,128)(2,1)} %copy.85), channel_id=1, source_target_pairs={{0,8},{4,12},{8,16},{12,20},{16,24},{20,28},{1,9},{5,13},{9,17},{1... | collective-permute-start | bytes 1572872 | tf_op jit(solution)/shard_map/ppermute | solution.py:27
  20.5 140.4 %collective-permute-start = (bf16[256,1024]{1,0:T(8,128)(2,1)S(1)}, bf16[256,1024]{1,0:T(8,128)(2,1)S(1)}, u32[]{:S(2)}, u32[]{:S(2)}) collective-permute-start(bf16[256,1024]{1,0:T(8,128)(2,1)S(1)} %copy-done.3), channel_id=1, source_target_pairs={{0,12},{4,16},{8,20},{12,24},{16,28},{1,13},{5,17},{9,21},{13,25},... | collective-permute-start | bytes 1572872 | tf_op jit(solution)/shard_map/ppermute | solution.py:27
  21.8 140.7 %collective-permute-start.1 = (bf16[256,1024]{1,0:T(8,128)(2,1)S(1)}, bf16[256,1024]{1,0:T(8,128)(2,1)S(1)}, u32[]{:S(2)}, u32[]{:S(2)}) collective-permute-start(bf16[256,1024]{1,0:T(8,128)(2,1)S(1)} %copy-done.3), channel_id=1, source_target_pairs={{0,8},{4,12},{8,16},{12,20},{16,24},{20,28},{1,9},{5,13},{9,17},{1... | collective-permute-start | bytes 1572872 | tf_op jit(solution)/shard_map/ppermute | solution.py:27
  23.1 140.2 %collective-permute-start.2 = (bf16[256,1024]{1,0:T(8,128)(2,1)S(1)}, bf16[256,1024]{1,0:T(8,128)(2,1)}, u32[]{:S(2)}, u32[]{:S(2)}) collective-permute-start(bf16[256,1024]{1,0:T(8,128)(2,1)S(1)} %copy-done.3), channel_id=1, source_target_pairs={{0,4},{4,8},{8,12},{12,16},{16,20},{20,24},{24,28},{1,5},{5,9},{9,... | collective-permute-start | bytes 1572872 | tf_op jit(solution)/shard_map/ppermute | solution.py:27
  160.9 1.6 copy-start.4
  160.9 13.4 %collective-permute-start.5 = (bf16[256,1024]{0,1:T(8,128)(2,1)}, bf16[256,1024]{0,1:T(8,128)(2,1)}, u32[]{:S(2)}, u32[]{:S(2)}) collective-permute-start(bf16[256,1024]{0,1:T(8,128)(2,1)} %copy.85), channel_id=1, source_target_pairs={{0,4},{4,8},{8,12},{12,16},{16,20},{20,24},{24,28},{1,5},{5,9},{9,... | collective-permute-start | bytes 1572872 | tf_op jit(solution)/shard_map/ppermute | solution.py:27
  162.5 0.8 copy-start.5
  177.9 1.7 copy-start.1
  182.9 10.1 %copy-start.2 = (bf16[256,1024]{1,0:T(8,128)(2,1)S(1)}, bf16[256,1024]{1,0:T(8,128)(2,1)}, u32[]{:S(2)}) copy-start(bf16[256,1024]{1,0:T(8,128)(2,1)} %param.15) | copy-start | bytes 1572868
  193.0 10.4 %copy-start.6 = (f32[1024]{0:T(1024)S(1)}, f32[1024]{0:T(1024)}, u32[]{:S(2)}) copy-start(f32[1024]{0:T(1024)} %param.18) | copy-start | bytes 12292
Sparse Core Ops, SparseCore 0:
  16.0 114.9 all-gather.3
where the time goes:
time: 213 us; the launch traced here: 212 us
  blocking collectives  142 us (67%)
  other arithmetic  19.3 us (9%)
  between operations  14.9 us (7%)
  local copies, waits for them, and re-layouts  10.9 us (5%)
  matrix products  10.4 us (5%)
  starting transfers between devices  7.77 us (4%)
  waiting for transfers between devices  6.78 us (3%)
    all_gather x1, blocking collectives, entering(): gathered = jax.tree.map(lambda a: lax.all_gather(a, axis), part)  136 us
    add x7, other arithmetic, combine(): latter[0][:, None, None] * former[1] + latter[1]  8.38 us
    ppermute x6, starting transfers between devices, from_behind(): return lax.ppermute(array, axis, pairs)  7.73 us
    ppermute x6, waiting for transfers between devices, from_behind(): return lax.ppermute(array, axis, pairs)  6.76 us
    psum x1, blocking collectives, shards(): norm_total = lax.psum(squares, 'head')  5.89 us
  transfers between devices with their start and end apart: 7, of which 1 were waited for; matrix products, arithmetic and copies ran while one was open for 7% of the time, Pallas kernels for 0%

commit v1 on v0

--- a/solution.py
+++ b/solution.py
@@ -89,7 +89,12 @@
     )
     mixture = inner_part + cross_part
     squares = jnp.sum(mixture * mixture, axis=(1, 2))
-    norm_total = lax.psum(squares, "head")
+
+    def treat_the_ticks(q_in):
+        shaped = jnp.sum(lax.all_gather(q_in, axis_name="head"), axis=0)
+        return shaped
+
+    norm_total = treat_the_ticks(squares)
     norm_scale = lax.rsqrt(norm_total / (HALF_MODEL_HEADS * HD) + 1e-06)
     lin_out = (
         mixture.reshape(token_rows, feature_width)

time: 213 us -> 213 us (level)
    psum x1 -> x0, blocking collectives: 5.89 us -> none  [shards(): norm_total = lax.psum(squares, 'head')]
    all_gather x0 -> x1, blocking collectives: none -> 5.07 us  [treat_the_ticks(): shaped = jnp.sum(lax.all_gather(q_in, axis_name='head'), axis=0)]
where the time goes in v1:
time: 213 us; the launch traced here: 212 us
  blocking collectives  141 us (66%)
  other arithmetic  19.3 us (9%)
  between operations  14.9 us (7%)
  local copies, waits for them, and re-layouts  10.9 us (5%)
  matrix products  10.4 us (5%)
  starting transfers between devices  7.77 us (4%)
  waiting for transfers between devices  6.78 us (3%)
    all_gather x1, blocking collectives, entering(): gathered = jax.tree.map(lambda a: lax.all_gather(a, axis), part)  136 us
    add x7, other arithmetic, combine(): latter[0][:, None, None] * former[1] + latter[1]  8.38 us
    ppermute x6, starting transfers between devices, from_behind(): return lax.ppermute(array, axis, pairs)  7.73 us
    ppermute x6, waiting for transfers between devices, from_behind(): return lax.ppermute(array, axis, pairs)  6.76 us
    all_gather x1, blocking collectives, treat_the_ticks(): shaped = jnp.sum(lax.all_gather(q_in, axis_name='head'), axis=0)  5.07 us
  transfers between devices with their start and end apart: 7, of which 1 were waited for; matrix products, arithmetic and copies ran while one was open for 7% of the time, Pallas kernels for 0%

profile of v1, /device:TPU:30, one launch (start us, length us, event | category | flops | bytes accessed | tf_op | source)
XLA Modules:
  0.0 211.6 jit_solution(15708293584865546018)
XLA Ops:
  10.7 1.3 reduce-window.6
  12.1 1.2 copy.96
  13.7 2.1 %fusion.22 = f32[8,128,128]{2,1,0:T(8,128)} fusion(bf16[256,8,128]{0,2,1:T(8,128)(2,1)S(1)} %bitcast.98, f32[256,8]{0,1:T(8,128)S(1)} %exponential_select_fusion.1, bf16[256,1024]{1,0:T(8,128)(2,1)} %param.15), kind=kOutput, calls=%fused_computation.30 | convolution fusion | flops 67895296 | bytes 1581056 | tf_op jit(solution)/shard_map/shd,she->hde/dot_general | solution.py:74
  15.9 2.1 copy.85
  17.9 1.3 collective-permute-start.3
  19.2 1.3 collective-permute-start.4
  20.5 1.3 collective-permute-start
  21.8 1.3 collective-permute-start.1
  23.1 1.3 collective-permute-start.2
  24.4 136.3 %all-gather.2 = f32[8,1,8]{2,1,0:T(1,128)S(1)} all-gather(f32[1,1,8]{2,1,0:T(1,128)S(1)} %bitcast.107), channel_id=1, replica_groups=mesh['seq'=8,'head'=4] {'seq'}, dimensions={0}, use_global_device_ids=true | all-gather | bytes 288 | tf_op jit(solution)/shard_map/all_gather | solution.py:13
  160.9 1.3 collective-permute-start.5
  163.3 1.7 pad_maximum_fusion
  165.0 2.6 %copy.84 = bf16[1024,1024]{0,1:T(8,128)(2,1)} copy(bf16[1024,1024]{1,0:T(8,128)(2,1)S(1)} %pad_maximum_fusion) | data formatting | bytes 4194304 | tf_op jit(solution)/shard_map/concatenate | solution.py:112
  167.6 6.7 %collective-permute-done.5 = bf16[256,1024]{0,1:T(8,128)(2,1)} collective-permute-done((bf16[256,1024]{0,1:T(8,128)(2,1)}, bf16[256,1024]{0,1:T(8,128)(2,1)}, u32[]{:S(2)}, u32[]{:S(2)}) %collective-permute-start.5) | collective-permute-done | bytes 524320 | tf_op jit(solution)/shard_map/ppermute | solution.py:27
  174.4 1.8 pad_maximum_fusion.1
  176.2 1.7 fusion.2
  177.9 1.7 fusion
  179.6 2.2 %divide_convert_fusion = bf16[256,8,128]{0,2,1:T(8,128)(2,1)S(1)} fusion(bf16[1024,8,128]{0,2,1:T(8,128)(2,1)S(1)} %bitcast.100, f32[8,1024,256]{2,1,0:T(8,128)S(1)} %get-tuple-element.74, f32[8,256]{1,0:T(8,128)S(1)} %get-tuple-element.73, pred[256,1024]{0,1:T(8,128)(4,1)S(1)} %compare_and_fusion, f32[256,8]{0,1:T(8,128)S(1)} %bitcast.105), kind=kOutput, calls=%fused_computation.21 | convolution fusion | flops 545783808 | bytes 11288576 | tf_op jit(solution)/shard_map/hts,shd->thd/dot_general | solution.py:127
  182.9 8.7 %while.12 = (s32[]{:T(128)}, f32[8,128,128]{2,1,0:T(8,128)S(1)}, s32[]{:T(128)}, f32[8,8]{1,0:T(8,128)S(1)}, f32[8,8,128,128]{3,2,1,0:T(8,128)}, /*index=5*/s32[]{:T(128)}, s32[]{:T(128)}, s32[]{:T(128)}) while((s32[]{:T(128)}, f32[8,128,128]{2,1,0:T(8,128)S(1)}, s32[]{:T(128)}, f32[8,8]{1,0:T(8,128)S(1)}, f32[8,8,128,128]{3,2,1,0:T(8,128)}, ...), condition=%wide.region_4.5_spmd, body=%wide.region_3.4_spmd.sunk | while | flops 262149 | bytes 1573087 | solution.py:21
  191.6 1.4 fusion.12
  193.0 2.9 %multiply_reduce_fusion = (f32[256]{0:T(256)S(1)}, f32[256,8,128]{0,2,1:T(8,128)}) fusion(f32[256,8,128]{0,2,1:T(8,128)S(1)} %fusion.12, bf16[256,8,128]{0,2,1:T(8,128)(2,1)S(1)} %bitcast.99, f32[8,256]{1,0:T(8,128)S(1)} %add_bitcast_fusion.1, pred[256,256]{1,0:T(8,128)(4,1)S(1)} %compare_and_fusion.1, bf16[256,1024]{1,0:T(8,128)(2,1)S(1)} %copy-done.2, ...), kind=kOutput, calls=%fused_computation.23 | convolution fusion | flops 271843072 | bytes 3744768 | tf_op jit(solution)/shard_map/hts,shd->thd/dot_general | solution.py:66
  195.9 1.6 copy.83
  197.5 5.1 %all-gather.3 = f32[4,1,256]{2,1,0:T(1,128)S(1)} all-gather(f32[1,1,256]{2,1,0:T(1,128)S(1)} %bitcast.108), channel_id=3, replica_groups=mesh['seq'=8,'head'=4] {'head'}, dimensions={0}, use_global_device_ids=true | all-gather | bytes 5120 | tf_op jit(solution)/shard_map/all_gather | solution.py:94
  202.6 2.2 %multiply_convert_fusion = bf16[256,1024]{1,0:T(8,128)(2,1)} fusion(bf16[256,1024]{1,0:T(8,128)(2,1)} %param.17, f32[256,1024]{1,0:T(8,128)S(1)} %copy.83, f32[1024]{0:T(1024)S(1)} %copy-done.6, f32[256]{0:T(256)S(1)} %add_rsqrt_fusion), kind=kLoop, calls=%fused_computation.22 | loop fusion | flops 2097152 | bytes 2102272 | tf_op jit(solution)/shard_map/convert_element_type | solution.py:104
  (55 shorter events, 14.2 us)
Async XLA Ops:
  7.2 169.0 %copy-start = (bf16[256,1024]{1,0:T(8,128)(2,1)S(1)}, bf16[256,1024]{1,0:T(8,128)(2,1)}, u32[]{:S(2)}) copy-start(bf16[256,1024]{1,0:T(8,128)(2,1)} %param.19) | copy-start | bytes 1572868
  7.2 13.3 %copy-start.3 = (bf16[256,1024]{1,0:T(8,128)(2,1)S(1)}, bf16[256,1024]{1,0:T(8,128)(2,1)}, u32[]{:S(2)}) copy-start(bf16[256,1024]{1,0:T(8,128)(2,1)} %param.21) | copy-start | bytes 1572868
  7.2 175.6 %all-gather.6.cloned.1.call-start = ((), (), s32[]{:S(2)}) async-start(), calls=%async_computation | async-start | bytes 4718592 | tf_op jit(solution)/shard_map/all_gather | solution.py:13
  17.9 149.7 %collective-permute-start.3 = (bf16[256,1024]{0,1:T(8,128)(2,1)}, bf16[256,1024]{0,1:T(8,128)(2,1)}, u32[]{:S(2)}, u32[]{:S(2)}) collective-permute-start(bf16[256,1024]{0,1:T(8,128)(2,1)} %copy.85), channel_id=1, source_target_pairs={{0,12},{4,16},{8,20},{12,24},{16,28},{1,13},{5,17},{9,21},{13,25},... | collective-permute-start | bytes 1572872 | tf_op jit(solution)/shard_map/ppermute | solution.py:27
  19.2 148.4 %collective-permute-start.4 = (bf16[256,1024]{0,1:T(8,128)(2,1)}, bf16[256,1024]{0,1:T(8,128)(2,1)}, u32[]{:S(2)}, u32[]{:S(2)}) collective-permute-start(bf16[256,1024]{0,1:T(8,128)(2,1)} %copy.85), channel_id=1, source_target_pairs={{0,8},{4,12},{8,16},{12,20},{16,24},{20,28},{1,9},{5,13},{9,17},{1... | collective-permute-start | bytes 1572872 | tf_op jit(solution)/shard_map/ppermute | solution.py:27
  20.5 140.4 %collective-permute-start = (bf16[256,1024]{1,0:T(8,128)(2,1)S(1)}, bf16[256,1024]{1,0:T(8,128)(2,1)S(1)}, u32[]{:S(2)}, u32[]{:S(2)}) collective-permute-start(bf16[256,1024]{1,0:T(8,128)(2,1)S(1)} %copy-done.3), channel_id=1, source_target_pairs={{0,12},{4,16},{8,20},{12,24},{16,28},{1,13},{5,17},{9,21},{13,25},... | collective-permute-start | bytes 1572872 | tf_op jit(solution)/shard_map/ppermute | solution.py:27
  21.8 140.7 %collective-permute-start.1 = (bf16[256,1024]{1,0:T(8,128)(2,1)S(1)}, bf16[256,1024]{1,0:T(8,128)(2,1)S(1)}, u32[]{:S(2)}, u32[]{:S(2)}) collective-permute-start(bf16[256,1024]{1,0:T(8,128)(2,1)S(1)} %copy-done.3), channel_id=1, source_target_pairs={{0,8},{4,12},{8,16},{12,20},{16,24},{20,28},{1,9},{5,13},{9,17},{1... | collective-permute-start | bytes 1572872 | tf_op jit(solution)/shard_map/ppermute | solution.py:27
  23.1 140.2 %collective-permute-start.2 = (bf16[256,1024]{1,0:T(8,128)(2,1)S(1)}, bf16[256,1024]{1,0:T(8,128)(2,1)}, u32[]{:S(2)}, u32[]{:S(2)}) collective-permute-start(bf16[256,1024]{1,0:T(8,128)(2,1)S(1)} %copy-done.3), channel_id=1, source_target_pairs={{0,4},{4,8},{8,12},{12,16},{16,20},{20,24},{24,28},{1,5},{5,9},{9,... | collective-permute-start | bytes 1572872 | tf_op jit(solution)/shard_map/ppermute | solution.py:27
  160.9 1.6 copy-start.4
  160.9 13.4 %collective-permute-start.5 = (bf16[256,1024]{0,1:T(8,128)(2,1)}, bf16[256,1024]{0,1:T(8,128)(2,1)}, u32[]{:S(2)}, u32[]{:S(2)}) collective-permute-start(bf16[256,1024]{0,1:T(8,128)(2,1)} %copy.85), channel_id=1, source_target_pairs={{0,4},{4,8},{8,12},{12,16},{16,20},{20,24},{24,28},{1,5},{5,9},{9,... | collective-permute-start | bytes 1572872 | tf_op jit(solution)/shard_map/ppermute | solution.py:27
  162.5 0.8 copy-start.5
  177.9 1.7 copy-start.1
  182.9 10.1 %copy-start.2 = (bf16[256,1024]{1,0:T(8,128)(2,1)S(1)}, bf16[256,1024]{1,0:T(8,128)(2,1)}, u32[]{:S(2)}) copy-start(bf16[256,1024]{1,0:T(8,128)(2,1)} %param.15) | copy-start | bytes 1572868
  193.0 9.6 %copy-start.6 = (f32[1024]{0:T(1024)S(1)}, f32[1024]{0:T(1024)}, u32[]{:S(2)}) copy-start(f32[1024]{0:T(1024)} %param.18) | copy-start | bytes 12292
Sparse Core Ops, SparseCore 0:
  16.0 114.9 all-gather.5
